TPU v7x, 128 devices: a whole 4x4x4 slice. The times are simulated.
128 devices in a mesh: dp: 32 (over z_lo, x, y), tensor: 4 (over z_hi, core).
Axes of the slice: x: 4, y: 4, z: 4 (z_hi: 2, z_lo: 2; z = z_hi * 2 + z_lo), core: 2. Of those that a mesh axis runs over, the one named last changes fastest.
Arguments:
- hidden: bfloat16 [64, 512, 5120], P('dp'), may hold values from -5 to 5
- query_projection_matrix: bfloat16 [5120, 2560], P('dp', 'tensor'), may hold values from -0.5 to 0.5
- key_projection_matrix: bfloat16 [5120, 2560], P('dp', 'tensor'), may hold values from -0.5 to 0.5
- value_projection_matrix: bfloat16 [5120, 2560], P('dp', 'tensor'), may hold values from -0.078125 to 0.078125
- adapter_down_maps: bfloat16 [2, 8, 5120], replicated, may hold values from -0.078125 to 0.078125
- adapter_up_maps: bfloat16 [2, 8, 2560], P(None, None, 'tensor'), may hold values from -1 to 1
- cotangent: bfloat16 [64, 512, 2560], P('dp', None, 'tensor'), may hold values from -6 to 6
- lengths: int32 [64], P('dp'), may hold values from 1 to 512, 16640 in all
- random_signs_down: bfloat16 [2, 8, 5120, 4096], P(None, None, ('dp', 'tensor')), may hold values from -4 to 4
- random_signs_up: bfloat16 [2, 8, 20, 128, 4096], P(None, None, 'tensor', 'dp'), may hold values from -4 to 4
Outputs:
- features: float32 [64, 4096], P('dp', 'tensor')
Inputs may be any that keep to these rules, and one draw needn't show every extreme that they name: `lengths`: positions at or beyond an example's length are padding.
All inputs are finite; a program needn't handle non-finite values. No bound on the sum of `lengths` on one device may be relied on, other than what follows from the above.
Results may differ from a plain program's by a relative error of at most 0.025.
Values may be sent and summed in bfloat16 or wider, within the bound.
A program may use at most 128 MiB of HBM per device.

v0:
```python
import jax
import jax.numpy as jnp
from jax import lax
from jax.sharding import Mesh, PartitionSpec as P

HEAD_DIM = 128
ADAPTER_RANK = 8
FEAT = 4096
DP_AXES = ("zl", "x", "y")
TP_AXES = ("zh", "core")
adapter_scale = 2.0
rope_base = 10000.0
norm_eps = 1e-05
masked_score = -1e30


def rope_tables(seq_len, head_width):
    half_width = head_width // 2
    frequency = rope_base ** (-2.0 * jnp.arange(half_width, dtype=jnp.float32) / head_width)
    angles = jnp.arange(seq_len, dtype=jnp.float32)[:, None] * frequency[None, :]
    rotary_cosines = jnp.concatenate([jnp.cos(angles), jnp.cos(angles)], axis=1)
    rotary_sines = jnp.concatenate([jnp.sin(angles), jnp.sin(angles)], axis=1)
    return (rotary_cosines, rotary_sines)


def apply_rotary(tensor_in, rotary_cosines, rotary_sines):
    half_width = tensor_in.shape[-1] // 2
    turned = jnp.concatenate([-tensor_in[..., half_width:], tensor_in[..., :half_width]], axis=-1)
    return tensor_in * rotary_cosines[:, None, :] + turned * rotary_sines[:, None, :]


def unrotate(gradient, rotary_cosines, rotary_sines):
    half_width = gradient.shape[-1] // 2
    scaled = gradient * rotary_sines[:, None, :]
    rotated_back = jnp.concatenate([scaled[..., half_width:], -scaled[..., :half_width]], axis=-1)
    return gradient * rotary_cosines[:, None, :] + rotated_back


def attention_grads(example):
    query_per_head, key_heads, value_per_head, grad_out, seq_length = example
    seq_len = query_per_head.shape[0]
    inv_root = query_per_head.shape[-1] ** (-0.5)
    scores = (
        jnp.einsum("qhc,khc->hqk", query_per_head, key_heads, preferred_element_type=jnp.float32)
        * inv_root
    )
    query_pos = jnp.arange(seq_len, dtype=jnp.int32)[:, None]
    key_pos = jnp.arange(seq_len, dtype=jnp.int32)[None, :]
    allowed = (key_pos <= query_pos) & (key_pos < seq_length)
    scores = jnp.where(allowed[None], scores, masked_score)
    row_max = jnp.max(scores, axis=-1, keepdims=True)
    expon = jnp.exp(scores - row_max)
    attention = expon / jnp.sum(expon, axis=-1, keepdims=True)
    attention_low = attention.astype(jnp.bfloat16)
    grad_values = jnp.einsum(
        "hqk,qhc->khc", attention_low, grad_out, preferred_element_type=jnp.float32
    )
    grad_attention = jnp.einsum(
        "qhc,khc->hqk", grad_out, value_per_head, preferred_element_type=jnp.float32
    )
    inner_sum = jnp.sum(attention * grad_attention, axis=-1, keepdims=True)
    grad_scores = (attention * (grad_attention - inner_sum)).astype(jnp.bfloat16)
    grad_query = (
        jnp.einsum("hqk,khc->qhc", grad_scores, key_heads, preferred_element_type=jnp.float32)
        * inv_root
    )
    return (grad_query, grad_values)


def body(
    hidden,
    query_projection_matrix,
    key_projection_matrix,
    value_projection_matrix,
    adapter_down_maps,
    adapter_up_maps,
    cotangent,
    lengths,
    random_signs_down,
    random_signs_up,
):
    seq_count, seq_len, model_width = hidden.shape
    local_cols = query_projection_matrix.shape[1]
    heads_local = local_cols // HEAD_DIM
    token_matrix = hidden.reshape(seq_count * seq_len, model_width)

    def add_rows(weight_piece):
        return jnp.dot(token_matrix, weight_piece, preferred_element_type=jnp.float32)

    parts_dp = lax.axis_size(DP_AXES)
    local_rows = jnp.concatenate(
        [query_projection_matrix, key_projection_matrix, value_projection_matrix], axis=1
    )
    partner_rows = lax.ppermute(local_rows, "zl", [(0, 1), (1, 0)])
    low_first = lax.axis_index("zl") == 0
    pair_rows = jnp.stack(
        [
            jnp.where(low_first, local_rows, partner_rows),
            jnp.where(low_first, partner_rows, local_rows),
        ]
    )
    all_rows = lax.all_gather(pair_rows, ("x", "y"), axis=1, tiled=False).reshape(
        -1, local_rows.shape[1]
    )
    projected = add_rows(all_rows)
    plain_query = projected[:, :local_cols]
    base_key = projected[:, local_cols : 2 * local_cols]
    plain_value = projected[:, 2 * local_cols :]
    rotary_cosines, rotary_sines = rope_tables(seq_len, HEAD_DIM)
    inner_hidden = jnp.einsum(
        "no,wio->nwi", token_matrix, adapter_down_maps, preferred_element_type=jnp.float32
    ).astype(jnp.bfloat16)
    raised_features = jnp.einsum(
        "kdg,dgj->kdj", inner_hidden, adapter_up_maps, preferred_element_type=jnp.float32
    )
    head_layout = (seq_count, seq_len, heads_local, HEAD_DIM)
    query_per_head = apply_rotary(
        (plain_query + adapter_scale * raised_features[:, 0]).reshape(head_layout),
        rotary_cosines,
        rotary_sines,
    ).astype(jnp.bfloat16)
    key_heads = apply_rotary(base_key.reshape(head_layout), rotary_cosines, rotary_sines).astype(
        jnp.bfloat16
    )
    value_per_head = (
        (plain_value + adapter_scale * raised_features[:, 1])
        .astype(jnp.bfloat16)
        .reshape(head_layout)
    )
    valid = jnp.arange(seq_len, dtype=jnp.int32)[None, :] < lengths[:, None]
    masked_out = jnp.where(valid[:, :, None], cotangent, jnp.zeros_like(cotangent)).reshape(
        head_layout
    )
    grad_query, grad_values = lax.map(
        attention_grads, (query_per_head, key_heads, value_per_head, masked_out, lengths)
    )
    grad_query = (
        unrotate(grad_query, rotary_cosines, rotary_sines)
        .astype(jnp.bfloat16)
        .reshape(seq_count, seq_len, local_cols)
    )
    grad_values = grad_values.astype(jnp.bfloat16).reshape(seq_count, seq_len, local_cols)
    per_head_gradient = jnp.stack([grad_query, grad_values], axis=2)
    branch_portion = jnp.einsum(
        "liov,ohv->lioh", per_head_gradient, adapter_up_maps, preferred_element_type=jnp.float32
    )
    adapter_branch = jnp.sum(
        lax.all_gather(branch_portion, TP_AXES, axis=0, tiled=False), axis=0
    ).astype(jnp.bfloat16)
    middle_seq = inner_hidden.reshape(seq_count, seq_len, 2, ADAPTER_RANK)
    up_map_gradient = adapter_scale * jnp.einsum(
        "esar,esac->earc", middle_seq, per_head_gradient, preferred_element_type=jnp.float32
    )
    parts_tensor = lax.axis_size(TP_AXES)
    row_block = model_width // (parts_dp * parts_tensor)
    hidden_blocks = hidden.reshape(seq_count, seq_len, parts_dp, parts_tensor, row_block)
    local_column_range = lax.dynamic_index_in_dim(
        hidden_blocks, lax.axis_index(TP_AXES), axis=3, keepdims=False
    )
    down_map_local = adapter_scale * jnp.einsum(
        "ykzu,ykhc->yhzuc", adapter_branch, local_column_range, preferred_element_type=jnp.float32
    )
    down_map_local = down_map_local.reshape(seq_count, parts_dp, 1, 2 * ADAPTER_RANK * row_block)
    slice_len = HEAD_DIM // parts_dp
    up_blocks = up_map_gradient.reshape(
        seq_count, 2, ADAPTER_RANK, heads_local, parts_dp, slice_len
    )
    up_blocks = up_blocks.transpose(0, 4, 1, 2, 3, 5).reshape(
        seq_count, parts_dp, 1, 2 * ADAPTER_RANK * heads_local * slice_len
    )
    packed = jnp.concatenate([down_map_local, up_blocks], axis=3).astype(jnp.bfloat16)
    routed = lax.all_to_all(packed, DP_AXES, split_axis=1, concat_axis=0, tiled=True)
    gathered = routed.reshape(routed.shape[0], routed.shape[3])
    down_count = down_map_local.shape[3]
    down_table = random_signs_down.reshape(down_count, random_signs_down.shape[-1])
    up_table = random_signs_up.reshape(gathered.shape[1] - down_count, random_signs_up.shape[-1])
    partial = (
        jnp.dot(gathered[:, :down_count], down_table, preferred_element_type=jnp.float32)
        + jnp.dot(gathered[:, down_count:], up_table, preferred_element_type=jnp.float32)
    ).astype(jnp.bfloat16)
    own_count = partial.shape[0] // parts_dp
    feat_block = partial.shape[1] // parts_tensor
    blocks = partial.reshape(parts_dp, own_count, parts_tensor, feat_block).transpose(0, 2, 1, 3)
    to_owner = lax.all_to_all(
        blocks.reshape(parts_dp * parts_tensor, own_count, feat_block),
        DP_AXES + TP_AXES,
        0,
        0,
        tiled=True,
    )
    features_local = jnp.sum(to_owner.astype(jnp.float32), axis=0)
    squares = lax.psum(jnp.sum(features_local * features_local, axis=1), TP_AXES)
    return features_local * lax.rsqrt(squares / FEAT + norm_eps)[:, None]


def solution(mesh):
    fine_mesh = Mesh(mesh.devices.reshape(2, 4, 4, 2, 2), ("zl", "x", "y", "zh", "core"))
    return jax.shard_map(
        body,
        mesh=fine_mesh,
        in_specs=(
            P(DP_AXES, None, None),
            P(DP_AXES, TP_AXES),
            P(DP_AXES, TP_AXES),
            P(DP_AXES, TP_AXES),
            P(),
            P(None, None, TP_AXES),
            P(DP_AXES, None, TP_AXES),
            P(DP_AXES),
            P(None, None, DP_AXES + TP_AXES, None),
            P(None, None, TP_AXES, DP_AXES, None),
        ),
        out_specs=P(DP_AXES, TP_AXES),
        check_vma=False,
    )
```

profile of v0, /device:TPU:0, one launch (start us, length us, event | category | flops | bytes accessed | tf_op | source)
XLA Modules:
  0.0 321.8 jit_solution(1688211024387175101)
XLA Ops:
  6.5 1.0 constant_dynamic-update-slice_fusion.2
  7.5 1.0 constant_dynamic-update-slice_fusion.1
  8.5 1.0 constant_dynamic-update-slice_fusion
  9.4 2.1 collective-permute-start
  11.6 13.9 %collective-permute-done = bf16[160,1920]{1,0:T(8,128)(2,1)S(1)} collective-permute-done((bf16[160,1920]{1,0:T(8,128)(2,1)S(1)}, bf16[160,1920]{1,0:T(8,128)(2,1)S(1)}, u32[]{:S(2)}, u32[]{:S(2)}) %collective-permute-start) | collective-permute-done | bytes 614432 | tf_op jit(solution)/shard_map/ppermute | solution.py:94
  25.5 1.2 pad_maximum_fusion.1
  26.8 0.7 copy.69
  27.4 14.0 %copy.61 = bf16[2,512,5120]{1,2,0:T(8,128)(2,1)} copy(bf16[2,512,5120]{2,1,0:T(8,128)(2,1)} %param.12) | data formatting | bytes 20971520 | tf_op args[0]
  41.4 0.5 fusion.71
  42.1 1.2 broadcast_select_fusion
  43.3 6.8 %convolution_convert_fusion = bf16[1024,2,8]{0,2,1:T(8,128)(2,1)S(1)} fusion(bf16[1024,5120,1]{1,0,2:T(8,128)(2,1)} %bitcast.140, bf16[2,8,5120]{2,1,0:T(8,128)(2,1)S(1)} %copy-done), kind=kOutput, calls=%fused_computation.79 | convolution fusion | flops 167788544 | bytes 10682368 | tf_op jit(solution)/shard_map/no,wio->nwi/dot_general | solution.py:110
  50.1 0.6 copy-done.12
  50.8 3.2 convolution_bitcast_fusion.1
  53.9 101.0 %all-gather.4.cloned.1.call-done = bf16[2,2560,1920]{2,1,0:T(8,128)(2,1)} async-done(((bf16[2,160,1920]{2,1,0:T(8,128)(2,1)}), bf16[2,2560,1920]{2,1,0:T(8,128)(2,1)}) %all-gather.4.cloned.1.call-update) | async-done | bytes 19660816 | tf_op jit(solution)/shard_map/all_gather | solution.py:102
  154.9 28.5 %convolution_bitcast_fusion = f32[1024,1920]{0,1:T(8,128)} fusion(bf16[5120,1920]{1,0:T(8,128)(2,1)} %bitcast.153, bf16[1024,5120]{1,0:T(8,128)(2,1)} %bitcast.141), kind=kOutput, calls=%fused_computation.44 | convolution fusion | flops 20132659200 | bytes 38010880 | tf_op jit(solution)/shard_map/dot_general | solution.py:88
  183.4 8.6 %fusion.42 = (bf16[1024,640]{0,1:T(8,128)(2,1)}, f32[1024,640]{0,1:T(8,128)}, f32[1024,640]{0,1:T(8,128)}) fusion(f32[1024,2,640]{0,2,1:T(8,128)} %convolution_bitcast_fusion.1, f32[1024,1920]{0,1:T(8,128)} %convolution_bitcast_fusion), kind=kLoop, calls=%fused_computation.48 | loop fusion | flops 3276800 | bytes 19660800 | tf_op jit(solution)/shard_map/convert_element_type | solution.py:127
  192.1 3.7 %reshape.155 = f32[2,512,5,128]{1,0,3,2:T(2,128)S(1)} reshape(f32[1024,640]{0,1:T(8,128)} %get-tuple-element.96) | data formatting | bytes 5242880 | tf_op jit(solution)/shard_map/reshape | solution.py:122
  195.7 2.0 copy.62
  197.7 4.8 %reshape.156 = f32[2,512,5,128]{1,0,3,2:T(2,128)} reshape(f32[1024,640]{0,1:T(8,128)} %get-tuple-element.95) | data formatting | bytes 5242880 | tf_op jit(solution)/shard_map/reshape | solution.py:118
  202.5 3.8 %copy.66 = f32[2,512,5,128]{1,3,2,0:T(8,128)} copy(f32[2,512,5,128]{1,0,3,2:T(2,128)} %reshape.156) | data formatting | bytes 5242880 | tf_op jit(solution)/shard_map/reshape | solution.py:118
  206.3 4.4 %reshape.158 = bf16[2,512,5,128]{1,0,3,2:T(2,128)(2,1)} reshape(bf16[1024,640]{0,1:T(8,128)(2,1)} %get-tuple-element.94) | data formatting | bytes 2621440 | tf_op jit(solution)/shard_map/reshape | solution.py:128
  210.7 4.3 %copy.73 = bf16[2,512,5,128]{3,1,2,0:T(8,128)(2,1)} copy(bf16[2,512,5,128]{1,0,3,2:T(2,128)(2,1)} %reshape.158) | data formatting | bytes 2621440 | tf_op jit(solution)/shard_map/while | solution.py:134
  215.0 3.4 %slice_negate_fusion.1 = (f32[2,512,5,64]{1,3,2,0:T(8,128)S(1)}, f32[2,512,5,64]{1,3,2,0:T(8,128)S(1)}, f32[2,512,5,64]{1,3,2,0:T(8,128)S(1)}, f32[2,512,5,64]{1,3,2,0:T(8,128)S(1)}) fusion(f32[2,512,5,128]{1,3,2,0:T(8,128)} %copy.66, f32[2,512,5,128]{1,3,2,0:T(8,128)} %copy.62), kind=kLoop, calls=%fused_computation.68 | loop fusion | flops 655360 | bytes 10485760 | tf_op jit(solution)/shard_map/neg | solution.py:28
  218.3 2.7 fusion.48
  221.0 22.2 %while.12 = (s32[]{:T(128)}, f32[2,512,5,128]{1,3,2,0:T(8,128)}, bf16[2,512,5,128]{1,3,2,0:T(8,128)(2,1)}, bf16[2,512,5,128]{1,3,2,0:T(8,128)(2,1)}, s32[2]{0:T(...) while((s32[]{:T(128)}, f32[2,512,5,128]{1,3,2,0:T(8,128)}, ...), condition=%wide.region_4.5_spmd, body=%wide.region_0.4_spmd.sunk | while | flops 1362688512 | bytes 75326712 | solution.py:134
  221.0 2.2 fusion.105
  223.2 0.6 dynamic_slice.73
  223.8 0.6 iota_compare_fusion.4
  224.6 2.5 fusion.107
  227.2 1.0 fusion.109
  228.2 0.3 copy-done.8
  228.5 0.8 multiply_reduce_fusion.3
  229.3 0.6 copy-done.3
  229.9 2.2 fusion.108
  232.2 2.2 fusion.105
  234.3 0.6 dynamic_slice.73
  235.0 0.6 iota_compare_fusion.4
  235.7 2.5 fusion.107
  238.3 1.0 fusion.109
  239.6 0.8 multiply_reduce_fusion.3
  240.5 0.6 copy-done.3
  241.1 2.2 fusion.108
  243.3 2.1 broadcast_multiply_fusion
  245.7 2.5 fusion.49
  248.2 1.4 copy.74
  249.6 1.5 copy.75
  251.1 2.1 convolution_bitcast_fusion.2
  253.2 7.5 %all-gather.1 = f32[8,512,2,8]{1,3,0,2:T(8,128)S(1)} all-gather(f32[2,512,2,8]{1,3,0,2:T(8,128)S(1)} %convolution_bitcast_fusion.2), channel_id=3, replica_groups=mesh['zl'=2,'x'=4,'y'=4,'zh'=2,'core'=2] {'zh','core'}, dimensions={0}, use_global_device_ids=true | all-gather | bytes 327680 | tf_op jit(solution)/shard_map/all_gather | solution.py:148
  260.7 3.3 %fusion.61 = bf16[2,32,2,8,40]{4,3,2,1,0:T(8,128)(2,1)S(1)} fusion(bf16[2,512,32,4,40]{1,4,3,2,0:T(8,128)(2,1)} %bitcast.142, s32[]{:T(128)S(6)} %select_n.24, bf16[2,512,2,8]{1,3,0,2:T(8,128)(2,1)S(1)} %reduce_sum.45), kind=kOutput, calls=%fused_computation.75 | convolution fusion | flops 42024960 | bytes 2736132 | tf_op jit(solution)/shard_map/ykzu,ykhc->yhzuc/dot_general | solution.py:160
  264.4 0.4 fusion.67
  264.8 0.3 copy.79
  265.1 0.4 copy.80
  265.7 0.8 pad_maximum_fusion.4
  266.5 6.4 %all-to-all-start = ((bf16[2,32,1,960]{3,0,2,1:T(2,128)(2,1)}), bf16[2,32,1,960]{3,0,2,1:T(2,128)(2,1)S(1)}, u32[]{:S(2)}, u32[]{:S(2)}) async-start(bf16[2,32,1,960]{3,0,2,1:T(2,128)(2,1)} %pad_maximum_fusion.4), calls=%async_computation | async-start | bytes 262144 | tf_op jit(solution)/shard_map/all_to_all | solution.py:172
  272.9 3.5 %reshape.163 = bf16[320,4096]{1,0:T(8,128)(2,1)S(1)} reshape(bf16[2,8,5,4,4096]{4,3,2,1,0:T(4,128)(2,1)} %param.21) | data formatting | bytes 5242880 | tf_op jit(solution)/shard_map/reshape | solution.py:176
  276.5 5.0 %all-to-all-done = bf16[2,32,1,960]{3,0,2,1:T(2,128)(2,1)S(1)} async-done(((bf16[2,32,1,960]{3,0,2,1:T(2,128)(2,1)}), bf16[2,32,1,960]{3,0,2,1:T(2,128)(2,1)S(1)}, u32[]{:S(2)}, u32[]{:S(2)}) %all-to-all-start) | async-done | bytes 122912 | tf_op jit(solution)/shard_map/all_to_all | solution.py:172
  281.6 3.5 %fusion.72 = f32[64,4096]{1,0:T(8,128)S(1)} fusion(bf16[640,4096]{1,0:T(8,128)(2,1)} %bitcast.143, bf16[64,960]{1,0:T(8,128)(2,1)S(1)} %reshape.161), kind=kOutput, calls=%fused_computation.89 | convolution fusion | flops 335544320 | bytes 6373376 | tf_op jit(solution)/shard_map/dot_general | solution.py:178
  285.1 0.7 fusion.39
  285.8 0.4 reshape.164
  286.2 0.5 copy.83
  286.7 18.9 %all_to_all.20 = bf16[128,2,1024]{2,1,0:T(2,128)(2,1)S(1)} all-to-all(bf16[128,2,1024]{2,1,0:T(2,128)(2,1)S(1)} %bitcast.146), channel_id=1, replica_groups=mesh['zl'=2,'x'=4,'y'=4,'zh'=2,'core'=2] {'zl','x','y','zh','core'}, dimensions={0} | all-to-all | bytes 1048576 | tf_op jit(solution)/shard_map/all_to_all | solution.py:184
  305.6 0.5 convert_reduce_fusion
  306.2 8.1 %psum.7 = f32[2]{0:T(128)S(1)} all-reduce(f32[2]{0:T(128)S(1)} %multiply_reduce_fusion.1), channel_id=1, replica_groups=mesh['zl'=2,'x'=4,'y'=4,'zh'=2,'core'=2] {'zh','core'}, use_global_device_ids=true, to_apply=%region_8.9 | all-reduce | flops 2 | bytes 16 | tf_op jit(solution)/shard_map/psum | solution.py:192
  314.3 0.7 broadcast_multiply_fusion.1
  (58 shorter events, 1.9 us)
Async XLA Ops:
  6.5 36.8 %copy-start = (bf16[2,8,5120]{2,1,0:T(8,128)(2,1)S(1)}, bf16[2,8,5120]{2,1,0:T(8,128)(2,1)}, u32[]{:S(2)}) copy-start(bf16[2,8,5120]{2,1,0:T(8,128)(2,1)} %param.16) | copy-start | bytes 491524
  6.5 148.4 %all-gather.4.cloned.1.call-start = ((), (), s32[]{:S(2)}) async-start(), calls=%async_computation.2 | async-start | bytes 20889600 | tf_op jit(solution)/shard_map/all_gather | solution.py:102
  9.4 16.0 %collective-permute-start = (bf16[160,1920]{1,0:T(8,128)(2,1)S(1)}, bf16[160,1920]{1,0:T(8,128)(2,1)S(1)}, u32[]{:S(2)}, u32[]{:S(2)}) collective-permute-start(bf16[160,1920]{1,0:T(8,128)(2,1)S(1)} %constant_dynamic-update-slice_fusion), channel_id=1, source_target_pairs={{0,64},{64,0},{1,65},{65,1},{2,66},{66,2},{3,67},{67,3},{4,68},{68... | collective-permute-start | bytes 1843208 | tf_op jit(solution)/shard_map/ppermute | solution.py:94
  11.6 15.2 %copy-start.4 = (bf16[2,512,640]{2,1,0:T(8,128)(2,1)S(1)}, bf16[2,512,640]{2,1,0:T(8,128)(2,1)}, u32[]{:S(2)}) copy-start(bf16[2,512,640]{2,1,0:T(8,128)(2,1)} %param.18) | copy-start | bytes 3932164
  27.4 14.6 %copy-start.16 = (s32[2]{0:T(128)S(1)}, s32[2]{0:T(128)}, u32[]{:S(2)}) copy-start(s32[2]{0:T(128)} %param.19) | copy-start | bytes 28
  43.3 7.4 %copy-start.14 = (bf16[2,8,640]{2,1,0:T(8,128)(2,1)S(1)}, bf16[2,8,640]{2,1,0:T(8,128)(2,1)}, u32[]{:S(2)}) copy-start(bf16[2,8,640]{2,1,0:T(8,128)(2,1)} %param.17) | copy-start | bytes 61444
  50.1 0.6 copy-start.12
  215.0 3.4 %copy-start.2 = (f32[2,512,5,128]{1,0,3,2:T(2,128)S(1)}, f32[2,512,5,128]{1,0,3,2:T(2,128)}, u32[]{:S(2)}) copy-start(f32[2,512,5,128]{1,0,3,2:T(2,128)} %reshape.156) | copy-start | bytes 7864324
  224.6 2.6 copy-start.5
  224.6 2.6 copy-start.11
  227.2 1.3 copy-start.8
  228.2 1.2 copy-start.6
  228.5 1.5 copy-start.3
  235.7 2.6 copy-start.5
  235.7 2.6 copy-start.11
  238.3 1.3 copy-start.8
  239.3 1.2 copy-start.6
  239.6 1.5 copy-start.3
  248.1 1.5 copy-start.7
  248.1 2.9 copy-start.15
  249.6 1.5 copy-start.9
  253.2 11.2 %copy-start.10 = (bf16[2,512,1,640]{3,1,0,2:T(8,128)(2,1)S(1)}, bf16[2,512,1,640]{3,1,0,2:T(8,128)(2,1)}, u32[]{:S(2)}) copy-start(bf16[2,512,1,640]{3,1,0,2:T(8,128)(2,1)} %copy.75) | copy-start | bytes 3932164
  253.2 11.2 %copy-start.13 = (bf16[1024,2,8]{0,2,1:T(8,128)(2,1)S(1)}, bf16[1024,2,8]{0,2,1:T(8,128)(2,1)}, u32[]{:S(2)}) copy-start(bf16[1024,2,8]{0,2,1:T(8,128)(2,1)} %copy-done.12) | copy-start | bytes 98308
  266.5 15.0 %all-to-all-start = ((bf16[2,32,1,960]{3,0,2,1:T(2,128)(2,1)}), bf16[2,32,1,960]{3,0,2,1:T(2,128)(2,1)S(1)}, u32[]{:S(2)}, u32[]{:S(2)}) async-start(bf16[2,32,1,960]{3,0,2,1:T(2,128)(2,1)} %pad_maximum_fusion.4), calls=%async_computation | async-start | bytes 262144 | tf_op jit(solution)/shard_map/all_to_all | solution.py:172
  285.1 29.9 %copy-start.1 = (bf16[2,8,5120]{2,1,0:T(8,128)(2,1)S(1)}, bf16[2,8,5120]{2,1,0:T(8,128)(2,1)}, u32[]{:S(2)}) copy-start(bf16[2,8,5120]{2,1,0:T(8,128)(2,1)} %param.16) | copy-start | bytes 491524
Sparse Core Ops, SparseCore 0:
  26.9 127.9 all-gather.3
where the time goes:
time: 323 us; the launch traced here: 322 us
  waiting for transfers between devices  120 us (37%)
  matrix products  61 us (19%)
  local copies, waits for them, and re-layouts  52.8 us (16%)
  blocking collectives  34.5 us (11%)
  other arithmetic  31.3 us (10%)
  between operations  13.7 us (4%)
  starting transfers between devices  8.52 us (3%)
    all_gather x1, waiting for transfers between devices, body(): lax.all_gather(pair_rows, ('x', 'y'), axis=1, tiled=False)  101 us
    dot_general x1, matrix products, add_rows(): jnp.dot(token_matrix, weight_piece, preferred_element_type=jnp.float32)  28.5 us
    all_to_all x1, blocking collectives, body(): lax.all_to_all(blocks.reshape(parts_dp * parts_tensor, own_count, feat_bl...  18.9 us
    unnamed x28, local copies, waits for them, and re-layouts  17.3 us
    ppermute x1, waiting for transfers between devices, body(): partner_rows = lax.ppermute(local_rows, 'zl', [(0, 1), (1, 0)])  13.9 us
    convert_element_type x1, other arithmetic, body(): value_per_head = (plain_value + adapter_scale * raised_features[:, 1]).as...  8.62 us
    reshape x2, local copies, waits for them, and re-layouts, body(): (plain_query + adapter_scale * raised_features[:, 0]).reshape(head_layout)  8.61 us
    psum x1, blocking collectives, body(): lax.psum(jnp.sum(features_local * features_local, axis=1), TP_AXES)  8.1 us
  transfers between devices with their start and end apart: 3, of which 3 were waited for; matrix products, arithmetic and copies ran while one was open for 9% of the time, Pallas kernels for 0%

commit v1 on v0

--- a/solution.py
+++ b/solution.py
@@ -169,7 +169,10 @@
         seq_count, parts_dp, 1, 2 * ADAPTER_RANK * heads_local * slice_len
     )
     packed = jnp.concatenate([down_map_local, up_blocks], axis=3).astype(jnp.bfloat16)
-    routed = lax.all_to_all(packed, DP_AXES, split_axis=1, concat_axis=0, tiled=True)
+    routed = jnp.concatenate(
+        lax.all_to_all(jnp.stack(jnp.split(packed, lax.axis_size(DP_AXES), axis=1)), DP_AXES, 0, 0),
+        axis=0,
+    )
     gathered = routed.reshape(routed.shape[0], routed.shape[3])
     down_count = down_map_local.shape[3]
     down_table = random_signs_down.reshape(down_count, random_signs_down.shape[-1])

time: 323 us -> 342 us (1.059)
  other arithmetic: 31.3 us -> 49.6 us
    unnamed x0 -> x31, other arithmetic: none -> 18.5 us
where the time goes in v1:
time: 342 us; the launch traced here: 340 us
  waiting for transfers between devices  120 us (35%)
  matrix products  61 us (18%)
  local copies, waits for them, and re-layouts  52.8 us (15%)
  other arithmetic  49.6 us (15%)
  blocking collectives  34.5 us (10%)
  between operations  13.7 us (4%)
  starting transfers between devices  8.52 us (2%)
    all_gather x1, waiting for transfers between devices, body(): lax.all_gather(pair_rows, ('x', 'y'), axis=1, tiled=False)  101 us
    dot_general x1, matrix products, add_rows(): jnp.dot(token_matrix, weight_piece, preferred_element_type=jnp.float32)  28.5 us
    all_to_all x1, blocking collectives, body(): lax.all_to_all(blocks.reshape(parts_dp * parts_tensor, own_count, feat_bl...  18.9 us
    unnamed x31, other arithmetic  18.5 us
    unnamed x28, local copies, waits for them, and re-layouts  17.3 us
    ppermute x1, waiting for transfers between devices, body(): partner_rows = lax.ppermute(local_rows, 'zl', [(0, 1), (1, 0)])  13.9 us
    convert_element_type x1, other arithmetic, body(): value_per_head = (plain_value + adapter_scale * raised_features[:, 1]).as...  8.62 us
    reshape x2, local copies, waits for them, and re-layouts, body(): (plain_query + adapter_scale * raised_features[:, 0]).reshape(head_layout)  8.61 us
  transfers between devices with their start and end apart: 3, of which 3 were waited for; matrix products, arithmetic and copies ran while one was open for 9% of the time, Pallas kernels for 0%

profile of v1, /device:TPU:0, one launch (start us, length us, event | category | flops | bytes accessed | tf_op | source)
XLA Modules:
  0.0 340.2 jit_solution(14164976010924299691)
XLA Ops:
  6.5 1.0 constant_dynamic-update-slice_fusion.2
  7.5 1.0 constant_dynamic-update-slice_fusion.1
  8.5 1.0 constant_dynamic-update-slice_fusion
  9.4 2.1 collective-permute-start
  11.6 13.9 %collective-permute-done = bf16[160,1920]{1,0:T(8,128)(2,1)S(1)} collective-permute-done((bf16[160,1920]{1,0:T(8,128)(2,1)S(1)}, bf16[160,1920]{1,0:T(8,128)(2,1)S(1)}, u32[]{:S(2)}, u32[]{:S(2)}) %collective-permute-start) | collective-permute-done | bytes 614432 | tf_op jit(solution)/shard_map/ppermute | solution.py:94
  25.5 1.2 pad_maximum_fusion.1
  26.8 0.7 copy.100
  27.4 14.0 %copy.92 = bf16[2,512,5120]{1,2,0:T(8,128)(2,1)} copy(bf16[2,512,5120]{2,1,0:T(8,128)(2,1)} %param.12) | data formatting | bytes 20971520 | tf_op args[0]
  42.1 1.2 broadcast_select_fusion
  43.3 6.8 %convolution_convert_fusion = bf16[1024,2,8]{0,2,1:T(8,128)(2,1)S(1)} fusion(bf16[1024,5120,1]{1,0,2:T(8,128)(2,1)} %bitcast.265, bf16[2,8,5120]{2,1,0:T(8,128)(2,1)S(1)} %copy-done), kind=kOutput, calls=%fused_computation.79 | convolution fusion | flops 167788544 | bytes 10682368 | tf_op jit(solution)/shard_map/no,wio->nwi/dot_general | solution.py:110
  50.1 0.6 copy-done.12
  50.8 3.2 convolution_bitcast_fusion.1
  53.9 101.0 %all-gather.4.cloned.1.call-done = bf16[2,2560,1920]{2,1,0:T(8,128)(2,1)} async-done(((bf16[2,160,1920]{2,1,0:T(8,128)(2,1)}), bf16[2,2560,1920]{2,1,0:T(8,128)(2,1)}) %all-gather.4.cloned.1.call-update) | async-done | bytes 19660816 | tf_op jit(solution)/shard_map/all_gather | solution.py:102
  154.9 28.5 %convolution_bitcast_fusion = f32[1024,1920]{0,1:T(8,128)} fusion(bf16[5120,1920]{1,0:T(8,128)(2,1)} %bitcast.277, bf16[1024,5120]{1,0:T(8,128)(2,1)} %bitcast.266), kind=kOutput, calls=%fused_computation.44 | convolution fusion | flops 20132659200 | bytes 38010880 | tf_op jit(solution)/shard_map/dot_general | solution.py:88
  183.4 8.6 %fusion.42 = (bf16[1024,640]{0,1:T(8,128)(2,1)}, f32[1024,640]{0,1:T(8,128)}, f32[1024,640]{0,1:T(8,128)}) fusion(f32[1024,2,640]{0,2,1:T(8,128)} %convolution_bitcast_fusion.1, f32[1024,1920]{0,1:T(8,128)} %convolution_bitcast_fusion), kind=kLoop, calls=%fused_computation.48 | loop fusion | flops 3276800 | bytes 19660800 | tf_op jit(solution)/shard_map/convert_element_type | solution.py:127
  192.1 3.7 %reshape.151 = f32[2,512,5,128]{1,0,3,2:T(2,128)S(1)} reshape(f32[1024,640]{0,1:T(8,128)} %get-tuple-element.96) | data formatting | bytes 5242880 | tf_op jit(solution)/shard_map/reshape | solution.py:122
  195.7 2.0 copy.93
  197.7 4.8 %reshape.152 = f32[2,512,5,128]{1,0,3,2:T(2,128)} reshape(f32[1024,640]{0,1:T(8,128)} %get-tuple-element.95) | data formatting | bytes 5242880 | tf_op jit(solution)/shard_map/reshape | solution.py:118
  202.5 3.8 %copy.97 = f32[2,512,5,128]{1,3,2,0:T(8,128)} copy(f32[2,512,5,128]{1,0,3,2:T(2,128)} %reshape.152) | data formatting | bytes 5242880 | tf_op jit(solution)/shard_map/reshape | solution.py:118
  206.3 4.4 %reshape.154 = bf16[2,512,5,128]{1,0,3,2:T(2,128)(2,1)} reshape(bf16[1024,640]{0,1:T(8,128)(2,1)} %get-tuple-element.94) | data formatting | bytes 2621440 | tf_op jit(solution)/shard_map/reshape | solution.py:128
  210.7 4.3 %copy.104 = bf16[2,512,5,128]{3,1,2,0:T(8,128)(2,1)} copy(bf16[2,512,5,128]{1,0,3,2:T(2,128)(2,1)} %reshape.154) | data formatting | bytes 2621440 | tf_op jit(solution)/shard_map/while | solution.py:134
  215.0 3.4 slice_negate_fusion.1
  218.3 2.7 fusion.48
  221.0 22.2 %while.12 = (s32[]{:T(128)}, f32[2,512,5,128]{1,3,2,0:T(8,128)}, bf16[2,512,5,128]{1,3,2,0:T(8,128)(2,1)}, bf16[2,512,5,128]{1,3,2,0:T(8,128)(2,1)}, s32[2]{0:T(...) while((s32[]{:T(128)}, f32[2,512,5,128]{1,3,2,0:T(8,128)}, ...), condition=%wide.region_4.5_spmd, body=%wide.region_0.4_spmd.sunk | while | flops 1362688512 | bytes 75326712 | solution.py:134
  221.0 2.2 fusion.106
  223.2 0.6 dynamic_slice.73
  223.8 0.6 iota_compare_fusion.4
  224.6 2.5 fusion.108
  227.2 1.0 fusion.110
  228.5 0.8 multiply_reduce_fusion.3
  229.3 0.6 copy-done.3
  229.9 2.2 fusion.109
  232.2 2.2 fusion.106
  234.3 0.6 dynamic_slice.73
  235.0 0.6 iota_compare_fusion.4
  235.7 2.5 fusion.108
  238.3 1.0 fusion.110
  239.6 0.8 multiply_reduce_fusion.3
  240.5 0.6 copy-done.3
  241.1 2.2 fusion.109
  243.3 2.1 broadcast_multiply_fusion
  245.7 2.5 fusion.49
  248.2 1.4 copy.105
  249.6 1.5 copy.106
  251.1 2.1 convolution_bitcast_fusion.2
  253.2 7.5 %all-gather.1 = f32[8,512,2,8]{1,3,0,2:T(8,128)S(1)} all-gather(f32[2,512,2,8]{1,3,0,2:T(8,128)S(1)} %convolution_bitcast_fusion.2), channel_id=3, replica_groups=mesh['zl'=2,'x'=4,'y'=4,'zh'=2,'core'=2] {'zh','core'}, dimensions={0}, use_global_device_ids=true | all-gather | bytes 327680 | tf_op jit(solution)/shard_map/all_gather | solution.py:148
  260.7 3.3 fusion.61
  266.3 0.6 constant_dynamic-update-slice_fusion.33
  268.7 0.6 constant_dynamic-update-slice_fusion.29
  271.7 0.6 constant_dynamic-update-slice_fusion.24
  275.3 0.6 constant_dynamic-update-slice_fusion.18
  277.7 0.6 constant_dynamic-update-slice_fusion.14
  281.3 0.6 constant_dynamic-update-slice_fusion.8
  281.9 0.6 constant_dynamic-update-slice_fusion.7
  283.7 0.6 constant_dynamic-update-slice_fusion.4
  284.3 0.6 constant_dynamic-update-slice_fusion.3
  284.9 6.4 %all-to-all-start = ((bf16[32,2,1,1,960]{4,1,3,2,0:T(2,128)(2,1)}), bf16[32,2,1,1,960]{4,1,3,2,0:T(2,128)(2,1)S(1)}, u32[]{:S(2)}, u32[]{:S(2)}) async-start(bf16[32,2,1,1,960]{4,1,3,2,0:T(2,128)(2,1)} %constant_dynamic-update-slice_fusion.3), calls=%async_computation | async-start | bytes 262144 | tf_op jit(solution)/shard_map/all_to_all | solution.py:173
  291.3 3.5 %reshape.158 = bf16[320,4096]{1,0:T(8,128)(2,1)S(1)} reshape(bf16[2,8,5,4,4096]{4,3,2,1,0:T(4,128)(2,1)} %param.21) | data formatting | bytes 5242880 | tf_op jit(solution)/shard_map/reshape | solution.py:179
  294.8 5.0 %all-to-all-done = bf16[32,2,1,1,960]{4,1,3,2,0:T(2,128)(2,1)S(1)} async-done(((bf16[32,2,1,1,960]{4,1,3,2,0:T(2,128)(2,1)}), bf16[32,2,1,1,960]{4,1,3,2,0:T(2,128)(2,1)S(1)}, u32[]{:S(2)}, u32[]{:S(2)}) %all-to-all-start) | async-done | bytes 122912 | tf_op jit(solution)/shard_map/all_to_all | solution.py:173
  299.9 3.5 %fusion.72 = f32[64,4096]{1,0:T(8,128)S(1)} fusion(bf16[640,4096]{1,0:T(8,128)(2,1)} %bitcast.268, bf16[64,960]{1,0:T(8,128)(2,1)S(1)} %reshape_reshape.3), kind=kOutput, calls=%fused_computation.88 | convolution fusion | flops 335544320 | bytes 6373376 | tf_op jit(solution)/shard_map/dot_general | solution.py:181
  303.5 0.7 fusion.39
  305.1 18.9 %all_to_all.10 = bf16[128,2,1024]{2,1,0:T(2,128)(2,1)S(1)} all-to-all(bf16[128,2,1024]{2,1,0:T(2,128)(2,1)S(1)} %bitcast.271), channel_id=1, replica_groups=mesh['zl'=2,'x'=4,'y'=4,'zh'=2,'core'=2] {'zl','x','y','zh','core'}, dimensions={0} | all-to-all | bytes 1048576 | tf_op jit(solution)/shard_map/all_to_all | solution.py:187
  324.6 8.1 %psum.7 = f32[2]{0:T(128)S(1)} all-reduce(f32[2]{0:T(128)S(1)} %multiply_reduce_fusion.1), channel_id=1, replica_groups=mesh['zl'=2,'x'=4,'y'=4,'zh'=2,'core'=2] {'zh','core'}, use_global_device_ids=true, to_apply=%region_8.9 | all-reduce | flops 2 | bytes 16 | tf_op jit(solution)/shard_map/psum | solution.py:195
  332.7 0.7 broadcast_multiply_fusion.1
  (89 shorter events, 19.0 us)
Async XLA Ops:
  6.5 36.8 %copy-start = (bf16[2,8,5120]{2,1,0:T(8,128)(2,1)S(1)}, bf16[2,8,5120]{2,1,0:T(8,128)(2,1)}, u32[]{:S(2)}) copy-start(bf16[2,8,5120]{2,1,0:T(8,128)(2,1)} %param.16) | copy-start | bytes 491524
  6.5 148.4 %all-gather.4.cloned.1.call-start = ((), (), s32[]{:S(2)}) async-start(), calls=%async_computation.2 | async-start | bytes 20889600 | tf_op jit(solution)/shard_map/all_gather | solution.py:102
  9.4 16.0 %collective-permute-start = (bf16[160,1920]{1,0:T(8,128)(2,1)S(1)}, bf16[160,1920]{1,0:T(8,128)(2,1)S(1)}, u32[]{:S(2)}, u32[]{:S(2)}) collective-permute-start(bf16[160,1920]{1,0:T(8,128)(2,1)S(1)} %constant_dynamic-update-slice_fusion), channel_id=1, source_target_pairs={{0,64},{64,0},{1,65},{65,1},{2,66},{66,2},{3,67},{67,3},{4,68},{68... | collective-permute-start | bytes 1843208 | tf_op jit(solution)/shard_map/ppermute | solution.py:94
  11.6 15.2 %copy-start.4 = (bf16[2,512,640]{2,1,0:T(8,128)(2,1)S(1)}, bf16[2,512,640]{2,1,0:T(8,128)(2,1)}, u32[]{:S(2)}) copy-start(bf16[2,512,640]{2,1,0:T(8,128)(2,1)} %param.18) | copy-start | bytes 3932164
  27.4 14.6 %copy-start.16 = (s32[2]{0:T(128)S(1)}, s32[2]{0:T(128)}, u32[]{:S(2)}) copy-start(s32[2]{0:T(128)} %param.19) | copy-start | bytes 28
  43.3 7.4 %copy-start.14 = (bf16[2,8,640]{2,1,0:T(8,128)(2,1)S(1)}, bf16[2,8,640]{2,1,0:T(8,128)(2,1)}, u32[]{:S(2)}) copy-start(bf16[2,8,640]{2,1,0:T(8,128)(2,1)} %param.17) | copy-start | bytes 61444
  50.1 0.6 copy-start.12
  215.0 3.4 copy-start.2
  224.6 2.6 copy-start.5
  224.6 2.6 copy-start.11
  227.2 1.3 copy-start.8
  228.2 1.2 copy-start.6
  228.5 1.5 copy-start.3
  235.7 2.6 copy-start.5
  235.7 2.6 copy-start.11
  238.3 1.3 copy-start.8
  239.3 1.2 copy-start.6
  239.6 1.5 copy-start.3
  248.1 1.5 copy-start.7
  248.1 2.9 copy-start.15
  249.6 1.5 copy-start.9
  253.2 11.2 %copy-start.10 = (bf16[2,512,1,640]{3,1,0,2:T(8,128)(2,1)S(1)}, bf16[2,512,1,640]{3,1,0,2:T(8,128)(2,1)}, u32[]{:S(2)}) copy-start(bf16[2,512,1,640]{3,1,0,2:T(8,128)(2,1)} %copy.106) | copy-start | bytes 3932164
  253.2 11.2 %copy-start.13 = (bf16[1024,2,8]{0,2,1:T(8,128)(2,1)S(1)}, bf16[1024,2,8]{0,2,1:T(8,128)(2,1)}, u32[]{:S(2)}) copy-start(bf16[1024,2,8]{0,2,1:T(8,128)(2,1)} %copy-done.12) | copy-start | bytes 98308
  284.9 15.0 %all-to-all-start = ((bf16[32,2,1,1,960]{4,1,3,2,0:T(2,128)(2,1)}), bf16[32,2,1,1,960]{4,1,3,2,0:T(2,128)(2,1)S(1)}, u32[]{:S(2)}, u32[]{:S(2)}) async-start(bf16[32,2,1,1,960]{4,1,3,2,0:T(2,128)(2,1)} %constant_dynamic-update-slice_fusion.3), calls=%async_computation | async-start | bytes 262144 | tf_op jit(solution)/shard_map/all_to_all | solution.py:173
  303.5 29.9 %copy-start.1 = (bf16[2,8,5120]{2,1,0:T(8,128)(2,1)S(1)}, bf16[2,8,5120]{2,1,0:T(8,128)(2,1)}, u32[]{:S(2)}) copy-start(bf16[2,8,5120]{2,1,0:T(8,128)(2,1)} %param.16) | copy-start | bytes 491524
Sparse Core Ops, SparseCore 0:
  26.9 127.9 all-gather.3
